TPU v7x, 32 devices: a whole 2x2x4 slice. The times are simulated.
32 devices in a mesh: grp: 2 (over x), tm: 16 (over z, y, core).
Axes of the slice: x: 2, y: 2, z: 4, core: 2. Of those that a mesh axis runs over, the one named last changes fastest.
Arguments:
- queries: bfloat16 [24576, 128], P(('grp', 'tm')), parts along dimension 0, may hold values from -6 to 6
- key_codes: bfloat16 [24576, 128], P(('grp', 'tm')), parts along dimension 0, may hold values from -6 to 6
- value_codes: bfloat16 [24576, 128], P(('grp', 'tm')), parts along dimension 0, may hold values from -6 to 6
- key_scales: float32 [192], P(('grp', 'tm')), parts along dimension 0, may hold values from 0.6 to 1.6
- value_scales: float32 [192], P(('grp', 'tm')), parts along dimension 0, may hold values from 0.3 to 3
- scale_slot: int32 [32, 6], P(('grp', 'tm')), parts along dimension 0, may hold values from 0 to 5, each once within a row
- grad_out: bfloat16 [24576, 128], P(('grp', 'tm')), parts along dimension 0, may hold values from -384 to 384
Outputs:
- query_grad: bfloat16 [24576, 128], P(('grp', 'tm')), parts along dimension 0
- key_grad: bfloat16 [24576, 128], P(('grp', 'tm')), parts along dimension 0
- value_grad: bfloat16 [24576, 128], P(('grp', 'tm')), parts along dimension 0
There are 2 independent parts, one for each index of `grp`. A program takes and returns all parts, laid end to end along the dimension named above; each array names one. Nothing has to cross between parts.
Inputs may be any that keep to these rules, and one draw needn't show every extreme that they name: Row s of scale_slot names every number 0 to 5 once.
All inputs are finite; a program needn't handle non-finite values.
Results may differ from a plain program's by a relative error of at most 0.0019.
The roundings to bfloat16 on the way count: a program that leaves them out, or rounds other values in their place, can miss the bound.
Values may be sent and summed in bfloat16 or wider, within the bound.
A program may use at most 64 MiB of HBM per device.

v0:
```python
import functools
import math

import jax
import jax.numpy as jnp
from jax import lax
from jax.experimental import pallas as pl
from jax.experimental.pallas import tpu as pltpu
from jax.sharding import PartitionSpec as P

HEAD_DIM = 128
TILE_TOKENS = 256
ROW_TILES = 4
CHIP_DEVICES = 2
KEY, VALUE, QUERY, GRAD = range(4)

MESH = pl.DeviceIdType.MESH
OFFSETS = ((0, 0), (0, -1), (0, 1), (-1, 0), (1, 0), (-1, -1), (-1, 1), (1, -1), (1, 1))
POSITION = {offset: position for position, offset in enumerate(OFFSETS)}
TURNS = ((0, 2, 1, 3, 4, 6, 8, 5, 7), (0, 1, 2, 3, 4, 5, 7, 6, 8))
STEPS = (
    (0, 0), (1, 0), (0, 1), (1, 1), (0, 2), (1, 2), (0, 3), (0, 4), (0, 5), (0, 6),
    (1, 3), (1, 4), (1, 5), (1, 6), (0, 7), (0, 8), (1, 7), (1, 8),
)
INVERSE = HEAD_DIM ** (-0.5)
LOG2_SCALE = INVERSE * math.log2(math.e)


def dot_nt(left, right):
    return lax.dot_general(left, right, (((1,), (1,)), ((), ())), preferred_element_type=jnp.float32)


def dot_tn(left, right):
    return lax.dot_general(left, right, (((0,), (0,)), ((), ())), preferred_element_type=jnp.float32)


def near_range(tile, tiles):
    return max(0, tile - 1) * TILE_TOKENS, min(tiles, tile + 2) * TILE_TOKENS


def chosen(position, part):
    value = jnp.int32(0)
    for index, offset in enumerate(OFFSETS):
        if offset[part]:
            value = jnp.where(position == index, jnp.int32(offset[part]), value)
    return value


def kernel(frames, rows, q_in, k_in, v_in, g_in, k_scales, v_scales, slot_in, dq_out, dk_out, dv_out,
           data, codes, stats, e_all, dp_all, m_rec, w_rec, m_run, l_run, w_run, dq_acc, dk_acc, dv_acc, dk_part, dv_part,
           in_sem, send_sem, recv_sem, st_send, st_recv):
    me = lax.axis_index("tm")
    frame, row = me // rows, me % rows
    tokens = q_in.shape[0]
    tiles = tokens // TILE_TOKENS

    def inside(frame_step, row_step):
        f, r = frame + frame_step, row + row_step
        return (f >= 0) & (f < frames) & (r >= 0) & (r < rows)

    def at_turn(turn):
        position = turn
        odd = row % CHIP_DEVICES == CHIP_DEVICES - 1
        for index in range(len(OFFSETS)):
            if TURNS[0][index] != index or TURNS[1][index] != index:
                slot = jnp.where(odd, jnp.int32(TURNS[1][index]), jnp.int32(TURNS[0][index]))
                position = jnp.where(turn == index, slot, position)
        return position

    def crossing(row_step):
        return jnp.minimum(row, row + row_step) % CHIP_DEVICES == CHIP_DEVICES - 1

    def neighbour(frame_step, row_step):
        return {"tm": me + frame_step * rows + row_step}

    loads = [
        pltpu.make_async_copy(source, target, in_sem.at[index])
        for index, (source, target) in enumerate(
            ((v_in, codes.at[0]), (k_in, codes.at[1]), (q_in, data.at[0, QUERY]), (g_in, data.at[0, GRAD]))
        )
    ]
    for load in loads:
        load.start()

    barrier = pltpu.get_barrier_semaphore()
    count = jnp.int32(0)
    for offset in OFFSETS[1:]:
        ok = inside(*offset)
        count = count + ok.astype(jnp.int32)

        @pl.when(ok)
        def _():
            pl.semaphore_signal(barrier, inc=1, device_id=neighbour(*offset), device_id_type=MESH)

    blocks = k_scales.shape[0]
    block = tokens // blocks
    for index, (part, scales) in enumerate(((VALUE, v_scales), (KEY, k_scales))):
        loads[index].wait()
        for place in range(blocks):
            span = pl.ds(place * block, block)
            scale = scales[slot_in[0, place]]
            data[0, part, span, :] = (codes[index, span, :].astype(jnp.float32) * scale).astype(jnp.bfloat16)
    for load in loads[2:]:
        load.wait()
    pl.semaphore_wait(barrier, count)

    def send(part, index, source, step):
        held = OFFSETS[source]
        target = POSITION[(held[0] - step[0], held[1] - step[1])]
        return pltpu.make_async_remote_copy(
            src_ref=data.at[source, part],
            dst_ref=data.at[target, part],
            send_sem=send_sem.at[part, index],
            recv_sem=recv_sem.at[part, target],
            device_id=neighbour(*step),
            device_id_type=MESH,
        )

    own_frame = ((0, 0, (-1, 0)), (1, 0, (1, 0)))
    own_row = ((2, 0, (0, -1)), (3, 0, (0, 1)))
    relay_row = ((4, 3, (0, -1)), (5, 3, (0, 1)), (6, 4, (0, -1)), (7, 4, (0, 1)))
    relay_frame = ((8, 1, (-1, 0)), (9, 1, (1, 0)), (10, 2, (-1, 0)), (11, 2, (1, 0)))

    def each(part, plans, action):
        for index, source, step in plans:
            held = OFFSETS[source]
            ok = inside(*step) & inside(*held)
            if source in (1, 2):
                if part in (KEY, QUERY):
                    continue
                ok = ok & crossing(held[1])
            elif source in (3, 4) and part in (VALUE, GRAD):
                ok = ok & jnp.logical_not(crossing(step[1]))

            @pl.when(ok)
            def _():
                action(send(part, index, source, step))

    def of(plans, source):
        return [plan for plan in plans if plan[1] == source]

    def start(copy):
        copy.start()

    each(VALUE, own_row, start)
    each(KEY, own_frame, start)
    each(KEY, own_row, start)
    each(VALUE, own_frame, start)
    each(GRAD, own_row, start)

    def arrived(part, position):
        step = (chosen(position, 0), chosen(position, 1))
        pltpu.make_async_remote_copy(
            src_ref=data.at[position, part],
            dst_ref=data.at[position, part],
            send_sem=send_sem.at[part, 0],
            recv_sem=recv_sem.at[part, position],
            device_id=neighbour(*step),
            device_id_type=MESH,
        ).wait_recv()

    def stats_arrived(position):
        step = (chosen(position, 0), chosen(position, 1))
        pltpu.make_async_remote_copy(
            src_ref=stats.at[position],
            dst_ref=stats.at[position],
            send_sem=st_send.at[0],
            recv_sem=st_recv.at[position],
            device_id=neighbour(*step),
            device_id_type=MESH,
        ).wait_recv()

    def forward(part, source, plans):
        @pl.when(inside(*OFFSETS[source]))
        def _():
            arrived(part, jnp.int32(source))
            each(part, of(plans, source), start)

    m_run[...] = jnp.full_like(m_run, -1e30)
    l_run[...] = jnp.zeros_like(l_run)
    w_run[...] = jnp.zeros_like(w_run)
    dq_acc[...] = jnp.zeros_like(dq_acc)
    dk_acc[...] = jnp.zeros_like(dk_acc)
    dv_acc[...] = jnp.zeros_like(dv_acc)

    starts, total = [], 0
    for tile in range(tiles):
        first, last = near_range(tile, tiles)
        starts.append(total)
        total += last - first

    def score_step(position):
        for tile in range(tiles):
            first, last = near_range(tile, tiles)
            own = pl.ds(tile * TILE_TOKENS, TILE_TOKENS)
            place = pl.ds(starts[tile], last - first)
            scores = dot_nt(data[position, KEY, first:last, :], data[0, QUERY, own, :]) * LOG2_SCALE
            old = m_run[:, own]
            new = jnp.maximum(old, jnp.max(scores, axis=0, keepdims=True))
            e = jnp.exp2(scores - new)
            m_run[:, own] = new
            m_rec[position, :, own] = new
            l_run[:, own] = l_run[:, own] * jnp.exp2(old - new) + jnp.sum(e, axis=0, keepdims=True)
            e_all[position, place, :] = e

    def value_step(position):
        for tile in range(tiles):
            first, last = near_range(tile, tiles)
            own = pl.ds(tile * TILE_TOKENS, TILE_TOKENS)
            place = pl.ds(starts[tile], last - first)
            grad_prob = dot_nt(data[position, VALUE, first:last, :], data[0, GRAD, own, :])
            w_rec[position, :, own] = jnp.sum(e_all[position, place, :] * grad_prob, axis=0, keepdims=True)
            dp_all[position, place, :] = grad_prob

    def stat_pass(step, carry):
        turn, is_value = jnp.int32(0), jnp.int32(0)
        for index, (with_value, which) in enumerate(STEPS):
            turn = jnp.where(step == index, jnp.int32(which), turn)
            is_value = jnp.where(step == index, jnp.int32(with_value), is_value)
        position = at_turn(turn)
        valid = inside(chosen(position, 0), chosen(position, 1))

        for source in (1, 2):
            @pl.when((position == source) & (is_value == 1))
            def _():
                forward(VALUE, source, relay_frame)

        @pl.when(step == STEPS.index((0, 3)))
        def _():
            for part in (QUERY, GRAD):
                each(part, own_frame, start)
            for source in (3, 4):
                forward(KEY, source, relay_row)
            each(QUERY, own_row, start)

        @pl.when(step == STEPS.index((1, 3)))
        def _():
            for source in (3, 4):
                forward(VALUE, source, relay_row)

        @pl.when(step == STEPS.index((0, 7)))
        def _():
            for source in (1, 2):
                forward(GRAD, source, relay_frame)

        @pl.when(valid & (is_value == 0))
        def _():
            @pl.when((position > 0) & (position != 3) & (position != 4))
            def _():
                arrived(KEY, position)

            score_step(position)

        @pl.when(valid & (is_value == 1))
        def _():
            @pl.when(position > 4)
            def _():
                arrived(VALUE, position)

            value_step(position)

        return carry

    lax.fori_loop(0, len(STEPS), stat_pass, 0)

    def weigh(position, carry):
        @pl.when(inside(chosen(position, 0), chosen(position, 1)))
        def _():
            w_run[...] += w_rec[position] * jnp.exp2(m_rec[position] - m_run[...])

        return carry

    lax.fori_loop(0, len(OFFSETS), weigh, 0)
    stats[0, 0:1, :] = m_run[...] + jnp.log2(l_run[...])
    stats[0, 1:2, :] = w_run[...] / l_run[...]

    def stats_send(index):
        offset = OFFSETS[index]
        back = POSITION[(-offset[0], -offset[1])]
        return pltpu.make_async_remote_copy(
            src_ref=stats.at[0],
            dst_ref=stats.at[back],
            send_sem=st_send.at[index],
            recv_sem=st_recv.at[back],
            device_id=neighbour(*offset),
            device_id_type=MESH,
        )

    def query_pass(position, carry):
        @pl.when(position == 1)
        def _():
            for index in range(1, len(OFFSETS)):
                @pl.when(inside(*OFFSETS[index]))
                def _():
                    stats_send(index).start()

        @pl.when(inside(chosen(position, 0), chosen(position, 1)))
        def _():
            for tile in range(tiles):
                first, last = near_range(tile, tiles)
                own = pl.ds(tile * TILE_TOKENS, TILE_TOKENS)
                place = pl.ds(starts[tile], last - first)
                factor = jnp.exp2(m_rec[position, :, own] - stats[0, 0:1, own])
                prob = e_all[position, place, :] * factor
                dscore = (prob * (dp_all[position, place, :] - stats[0, 1:2, own])).astype(jnp.bfloat16)
                dq_acc[:, own] += dot_tn(data[position, KEY, first:last, :], dscore)

        return carry

    lax.fori_loop(0, len(OFFSETS), query_pass, 0)
    dq_out[...] = (dq_acc[...].T * INVERSE).astype(dq_out.dtype)

    def key_parts(position, known):
        done = 0
        for tile in range(tiles):
            first, last = near_range(tile, tiles)
            own = pl.ds(tile * TILE_TOKENS, TILE_TOKENS)
            query = data[position, QUERY, own, :]
            grad = data[position, GRAD, own, :]
            if known:
                place = pl.ds(starts[tile], last - first)
                prob = e_all[0, place, :] * jnp.exp2(m_rec[0, :, own] - stats[0, 0:1, own])
                grad_prob = dp_all[0, place, :]
            else:
                scores = dot_nt(data[0, KEY, first:last, :], query) * LOG2_SCALE
                prob = jnp.exp2(scores - stats[position, 0:1, own])
                grad_prob = dot_nt(data[0, VALUE, first:last, :], grad)
            dscore = (prob * (grad_prob - stats[position, 1:2, own])).astype(jnp.bfloat16)
            key_part = jnp.dot(dscore, query, preferred_element_type=jnp.float32)
            value_part = jnp.dot(prob.astype(jnp.bfloat16), grad, preferred_element_type=jnp.float32)
            if first < done:
                dk_part[first:done, :] += key_part[:done - first]
                dv_part[first:done, :] += value_part[:done - first]
            if done < last:
                dk_part[done:last, :] = key_part[done - first:]
                dv_part[done:last, :] = value_part[done - first:]
            done = last

    for source in (3, 4):
        forward(QUERY, source, relay_row)

    def key_pass(turn, carry):
        position = at_turn(turn)

        @pl.when(turn == 3)
        def _():
            for source in (3, 4):
                forward(GRAD, source, relay_row)

        @pl.when(inside(chosen(position, 0), chosen(position, 1)))
        def _():
            @pl.when(position > 0)
            def _():
                stats_arrived(position)

            @pl.when((position > 0) & (position != 3) & (position != 4))
            def _():
                arrived(QUERY, position)

            @pl.when(position > 4)
            def _():
                arrived(GRAD, position)

            @pl.when(position == 0)
            def _():
                key_parts(position, True)

            @pl.when(position > 0)
            def _():
                key_parts(position, False)

            key_part = (dk_part[...] * INVERSE).astype(jnp.bfloat16)
            dk_acc[...] += key_part.astype(jnp.float32)
            dv_acc[...] += dv_part[...].astype(jnp.bfloat16).astype(jnp.float32)

        return carry

    lax.fori_loop(0, len(OFFSETS), key_pass, 0)
    dk_out[...] = dk_acc[...].astype(dk_out.dtype)
    dv_out[...] = dv_acc[...].astype(dv_out.dtype)

    def sent(copy):
        copy.wait_send()

    for part in (KEY, VALUE, QUERY, GRAD):
        each(part, own_frame + own_row + relay_row + relay_frame, sent)
    for index in range(1, len(OFFSETS)):
        @pl.when(inside(*OFFSETS[index]))
        def _():
            stats_send(index).wait_send()


def put_out(dq_in, dk_in, dv_in, dq_out, dk_out, dv_out, held, in_sem, out_sem):
    pairs = ((dq_in, dq_out), (dk_in, dk_out), (dv_in, dv_out))
    loads = [pltpu.make_async_copy(pair[0], held.at[i], in_sem.at[i]) for i, pair in enumerate(pairs)]
    stores = [pltpu.make_async_copy(held.at[i], pair[1], out_sem.at[i]) for i, pair in enumerate(pairs)]
    for load in loads:
        load.start()
    for load, store in zip(loads, stores):
        load.wait()
        store.start()
    for store in stores:
        store.wait()


def per_device(queries, key_codes, value_codes, key_scales, value_scales, scale_slot, grad_out):
    rows = ROW_TILES
    frames = lax.axis_size("tm") // rows
    tokens, head_dim = queries.shape
    tiles = tokens // TILE_TOKENS
    near = sum(near_range(tile, tiles)[1] - near_range(tile, tiles)[0] for tile in range(tiles))
    slots = len(OFFSETS)
    shape = jax.ShapeDtypeStruct((tokens, head_dim), jnp.bfloat16)
    grads = pl.pallas_call(
        functools.partial(kernel, frames, rows),
        out_shape=(shape, shape, shape),
        in_specs=[pl.BlockSpec(memory_space=pl.ANY)] * 4 + [pl.BlockSpec(memory_space=pltpu.SMEM)] * 3,
        out_specs=[pl.BlockSpec(memory_space=pltpu.VMEM)] * 3,
        scratch_shapes=[
            pltpu.VMEM((slots, 4, tokens, head_dim), jnp.bfloat16),
            pltpu.VMEM((2, tokens, head_dim), jnp.bfloat16),
            pltpu.VMEM((slots, 2, tokens), jnp.float32),
            pltpu.VMEM((slots, near, TILE_TOKENS), jnp.float32),
            pltpu.VMEM((slots, near, TILE_TOKENS), jnp.float32),
            pltpu.VMEM((slots, 1, tokens), jnp.float32),
            pltpu.VMEM((slots, 1, tokens), jnp.float32),
            pltpu.VMEM((1, tokens), jnp.float32),
            pltpu.VMEM((1, tokens), jnp.float32),
            pltpu.VMEM((1, tokens), jnp.float32),
            pltpu.VMEM((head_dim, tokens), jnp.float32),
            pltpu.VMEM((tokens, head_dim), jnp.float32),
            pltpu.VMEM((tokens, head_dim), jnp.float32),
            pltpu.VMEM((tokens, head_dim), jnp.float32),
            pltpu.VMEM((tokens, head_dim), jnp.float32),
            pltpu.SemaphoreType.DMA((4,)),
            pltpu.SemaphoreType.DMA((4, 12)),
            pltpu.SemaphoreType.DMA((4, slots)),
            pltpu.SemaphoreType.DMA((slots,)),
            pltpu.SemaphoreType.DMA((slots,)),
        ],
        compiler_params=pltpu.CompilerParams(
            collective_id=0, has_side_effects=True, vmem_limit_bytes=60 * 1024 * 1024
        ),
    )(queries, key_codes, value_codes, grad_out, key_scales, value_scales, scale_slot)
    return tuple(pl.pallas_call(
        put_out,
        out_shape=(shape, shape, shape),
        in_specs=[pl.BlockSpec(memory_space=pl.ANY)] * 3,
        out_specs=[pl.BlockSpec(memory_space=pl.ANY)] * 3,
        scratch_shapes=[
            pltpu.VMEM((3, tokens, head_dim), jnp.bfloat16),
            pltpu.SemaphoreType.DMA((3,)),
            pltpu.SemaphoreType.DMA((3,)),
        ],
        compiler_params=pltpu.CompilerParams(vmem_limit_bytes=60 * 1024 * 1024),
    )(*grads))


def solution(mesh):
    in_specs = (
        P(("grp", "tm"), None),
        P(("grp", "tm"), None),
        P(("grp", "tm"), None),
        P(("grp", "tm")),
        P(("grp", "tm")),
        P(("grp", "tm"), None),
        P(("grp", "tm"), None),
    )
    out_specs = (P(("grp", "tm"), None), P(("grp", "tm"), None), P(("grp", "tm"), None))
    return jax.shard_map(
        per_device, mesh=mesh, in_specs=in_specs, out_specs=out_specs, check_vma=False
    )
```

profile of v0, /device:TPU:9, one launch (start us, length us, event | category | flops | bytes accessed | tf_op | source)
XLA Modules:
  0.0 39.2 jit_solution(11340047589532195908)
XLA Ops:
  0.6 36.7 %shard_map.94 = (bf16[768,128]{1,0:T(8,128)(2,1)}, bf16[768,128]{1,0:T(8,128)(2,1)}, bf16[768,128]{1,0:T(8,128)(2,1)}) custom-call(bf16[768,128]{1,0:T(8,128)(2,1)} %q_in.1, bf16[768,128]{1,0:T(8,128)(2,1)} %k_in.1, bf16[768,128]{1,0:T(8,128)(2,1)} %v_in.1, bf16[768,128]{1,0:T(8,128)(2,1)} %g_in.1, f32[6]{0:T(128)} %k_scales.1, f32[6]{0:T(128)} %v_scales.1, ...), custom_call_target="tpu_custom_call" | custom-call | tf_op jit(solution)/shard_map/pallas_call | solution.py:414
  37.4 1.8 %shard_map.95 = (bf16[768,128]{1,0:T(8,128)(2,1)}, bf16[768,128]{1,0:T(8,128)(2,1)}, bf16[768,128]{1,0:T(8,128)(2,1)}) custom-call(bf16[768,128]{1,0:T(8,128)(2,1)} %get-tuple-element.6.dq_in, bf16[768,128]{1,0:T(8,128)(2,1)} %get-tuple-element.7.dk_in, bf16[768,128]{1,0:T(8,128)(2,1)} %get-tuple-element.8.dv_in), custom_call_target="tpu_custom_call" | custom-call | tf_op jit(solution)/shard_map/pallas_call | solution.py:445
where the time goes:
time: 39.4 us; the launch traced here: 39.2 us
  Pallas kernels  38.6 us (98%)
  between operations  0.64 us (2%)
    pallas_call x1, Pallas kernels, per_device(): pl.pallas_call(functools.partial(kernel, frames, rows), out_shape=(shape,...  36.7 us
    pallas_call x1, Pallas kernels, per_device(): pl.pallas_call(put_out, out_shape=(shape, shape, shape), in_specs=[pl.Blo...  1.84 us

commit v1 on v0

--- a/solution.py
+++ b/solution.py
@@ -390,14 +390,10 @@
             stats_send(index).wait_send()
 
 
-def put_out(dq_in, dk_in, dv_in, dq_out, dk_out, dv_out, held, in_sem, out_sem):
+def put_out(dq_in, dk_in, dv_in, dq_out, dk_out, dv_out, out_sem):
     pairs = ((dq_in, dq_out), (dk_in, dk_out), (dv_in, dv_out))
-    loads = [pltpu.make_async_copy(pair[0], held.at[i], in_sem.at[i]) for i, pair in enumerate(pairs)]
-    stores = [pltpu.make_async_copy(held.at[i], pair[1], out_sem.at[i]) for i, pair in enumerate(pairs)]
-    for load in loads:
-        load.start()
-    for load, store in zip(loads, stores):
-        load.wait()
+    stores = [pltpu.make_async_copy(pair[0], pair[1], out_sem.at[i]) for i, pair in enumerate(pairs)]
+    for store in stores:
         store.start()
     for store in stores:
         store.wait()
@@ -413,8 +409,8 @@
     shape = jax.ShapeDtypeStruct((tokens, head_dim), jnp.bfloat16)
     grads = pl.pallas_call(
         functools.partial(kernel, frames, rows),
-        out_shape=(shape, shape, shape),
-        in_specs=[pl.BlockSpec(memory_space=pl.ANY)] * 4 + [pl.BlockSpec(memory_space=pltpu.SMEM)] * 3,
+        out_shape=(pltpu.VMEM((tokens, head_dim), jnp.bfloat16),) * 3,
+        in_specs=[pl.BlockSpec(memory_space=pltpu.HBM)] * 4 + [pl.BlockSpec(memory_space=pltpu.SMEM)] * 3,
         out_specs=[pl.BlockSpec(memory_space=pltpu.VMEM)] * 3,
         scratch_shapes=[
             pltpu.VMEM((slots, 4, tokens, head_dim), jnp.bfloat16),
@@ -445,14 +441,10 @@
     return tuple(pl.pallas_call(
         put_out,
         out_shape=(shape, shape, shape),
-        in_specs=[pl.BlockSpec(memory_space=pl.ANY)] * 3,
+        in_specs=[pl.BlockSpec(memory_space=pltpu.VMEM)] * 3,
         out_specs=[pl.BlockSpec(memory_space=pl.ANY)] * 3,
-        scratch_shapes=[
-            pltpu.VMEM((3, tokens, head_dim), jnp.bfloat16),
-            pltpu.SemaphoreType.DMA((3,)),
-            pltpu.SemaphoreType.DMA((3,)),
-        ],
-        compiler_params=pltpu.CompilerParams(vmem_limit_bytes=60 * 1024 * 1024),
+        scratch_shapes=[pltpu.SemaphoreType.DMA((3,))],
+        compiler_params=pltpu.CompilerParams(vmem_limit_bytes=2 * 1024 * 1024),
     )(*grads))
 
 

time: 39.4 us -> 37.5 us (0.952)
  Pallas kernels: 38.6 us -> 36.7 us
    pallas_call x1, Pallas kernels: 1.84 us -> 0.83 us  [per_device(): pl.pallas_call(put_out, out_shape=(shape, shape, shape), in_specs=[pl.Blo...]
    pallas_call x1, Pallas kernels: 36.7 us -> 35.9 us  [per_device(): pl.pallas_call(functools.partial(kernel, frames, rows), out_shape=(pltpu....]
where the time goes in v1:
time: 37.5 us; the launch traced here: 37.4 us
  Pallas kernels  36.7 us (98%)
  between operations  0.64 us (2%)
    pallas_call x1, Pallas kernels, per_device(): pl.pallas_call(functools.partial(kernel, frames, rows), out_shape=(pltpu....  35.9 us
    pallas_call x1, Pallas kernels, per_device(): pl.pallas_call(put_out, out_shape=(shape, shape, shape), in_specs=[pl.Blo...  0.83 us

profile of v1, /device:TPU:9, one launch (start us, length us, event | category | flops | bytes accessed | tf_op | source)
XLA Modules:
  0.0 37.4 jit_solution(6039624174672506158)
XLA Ops:
  0.6 35.9 %shard_map.94 = (bf16[768,128]{1,0:T(8,128)(2,1)S(1)}, bf16[768,128]{1,0:T(8,128)(2,1)S(1)}, bf16[768,128]{1,0:T(8,128)(2,1)S(1)}) custom-call(bf16[768,128]{1,0:T(8,128)(2,1)} %q_in.1, bf16[768,128]{1,0:T(8,128)(2,1)} %k_in.1, bf16[768,128]{1,0:T(8,128)(2,1)} %v_in.1, bf16[768,128]{1,0:T(8,128)(2,1)} %g_in.1, f32[6]{0:T(128)} %k_scales.1, f32[6]{0:T(128)} %v_scales.1, ...), custom_call_target="tpu_custom_call" | custom-call | tf_op jit(solution)/shard_map/pallas_call | solution.py:410
  36.5 0.8 %shard_map.95 = (bf16[768,128]{1,0:T(8,128)(2,1)}, bf16[768,128]{1,0:T(8,128)(2,1)}, bf16[768,128]{1,0:T(8,128)(2,1)}) custom-call(bf16[768,128]{1,0:T(8,128)(2,1)S(1)} %get-tuple-element.6.dq_in, bf16[768,128]{1,0:T(8,128)(2,1)S(1)} %get-tuple-element.7.dk_in, bf16[768,128]{1,0:T(8,128)(2,1)S(1)} %get-tuple-element.8.dv_in), custom_call_target="tpu_custom_call" | custom-call | tf_op jit(solution)/shard_map/pallas_call | solution.py:441

commit v2 on v1

v2 whole, which is shorter than its diff:
```python
import functools
import math

import jax
import jax.numpy as jnp
from jax import lax
from jax.experimental import pallas as pl
from jax.experimental.pallas import tpu as pltpu
from jax.sharding import PartitionSpec as P

HEAD_DIM = 128
TILE_TOKENS = 256
ROW_TILES = 4
CHIP_DEVICES = 2
KEY, VALUE, QUERY, GRAD = range(4)

MESH = pl.DeviceIdType.MESH
INVERSE = HEAD_DIM ** (-0.5)
LOG2_SCALE = INVERSE * math.log2(math.e)

OWN, C, X, AM, AZ, BM, BZ, MX, ZX = range(9)
SLOTS = 9
NAMES = ("", "C", "X", "AM", "AZ", "BM", "BZ", "MX", "ZX")


def dot_nt(left, right):
    return lax.dot_general(left, right, (((1,), (1,)), ((), ())), preferred_element_type=jnp.float32)


def near_range(tile, tiles):
    return max(0, tile - 1) * TILE_TOKENS, min(tiles, tile + 2) * TILE_TOKENS


def kernel(frames, rows, q_in, k_in, v_in, g_in, k_scales, v_scales, slot_in, dq_out, dk_out, dv_out,
           data, codes, stats, e_all, dp_all, ps, ds, m_rec, w_rec, l_rec, dq_acc, dk_acc, dv_acc,
           part_out, part_in, in_sem, send_sem, recv_sem, st_send, st_recv, pt_send, pt_recv):
    me = lax.axis_index("tm")
    frame, row = me // rows, me % rows
    tokens = q_in.shape[0]
    tiles = tokens // TILE_TOKENS
    turn = 1 - 2 * (row % CHIP_DEVICES)

    inner = (row - turn >= 0) & (row - turn < rows)
    has = {"C": None, "A": None, "B": None, "X": inner, "M": frame > 0, "Z": frame < frames - 1}
    outer = jnp.logical_not(inner)
    shift = {
        "C": turn, "X": -turn, "M": -rows, "Z": rows,
        "A": jnp.where(inner, 0, turn), "B": jnp.where(inner, turn, 0),
    }
    names = NAMES

    def valid(text):
        ok = None
        for name in text:
            if has[name] is not None:
                ok = has[name] if ok is None else ok & has[name]
        return ok

    def device(text):
        return {"tm": me + sum(shift[name] for name in text)}

    def lands(source, way):
        if source == OWN and way in "MZ":
            return jnp.where(inner, AZ, BZ) if way == "M" else jnp.where(inner, AM, BM)
        fixed = {
            (OWN, "C"): C, (OWN, "X"): X, (AM, "X"): MX, (AZ, "X"): ZX, (X, "Z"): MX, (X, "M"): ZX,
        }
        return source if way == "C" and source != OWN else fixed[source, way]

    def guard(ok, action):
        if ok is None:
            action()
        else:
            pl.when(ok)(action)

    def masked(slot, value, other):
        ok = valid(names[slot])
        return value if ok is None else jnp.where(ok, value, other)

    def across(slot, value):
        return masked(slot, value, 0.0) if slot in (X, MX, ZX) else value

    def inner_rows(action):
        pl.when(inner)(action)

    loads = [
        pltpu.make_async_copy(source, target, in_sem.at[index])
        for index, (source, target) in enumerate(
            ((k_in, codes.at[0]), (v_in, codes.at[1]), (q_in, data.at[OWN, QUERY]), (g_in, data.at[OWN, GRAD]))
        )
    ]
    for load in loads:
        load.start()

    barrier = pltpu.get_barrier_semaphore()
    count = jnp.int32(1)
    for slot in range(1, SLOTS):
        ok = valid(names[slot])
        if ok is not None:
            count = count + ok.astype(jnp.int32)

        def greet():
            pl.semaphore_signal(barrier, inc=1, device_id=device(names[slot]), device_id_type=MESH)

        guard(ok, greet)

    for name, slots in (("M", (AM, BM)), ("Z", (AZ, BZ))):
        @pl.when(jnp.logical_not(has[name]))
        def _():
            for slot in slots:
                data[slot] = jnp.zeros_like(data[slot])
                stats[slot] = jnp.zeros_like(stats[slot])

    @pl.when(outer)
    def _():
        for slot in (X, MX, ZX):
            m_rec[slot] = jnp.full_like(m_rec[slot], -1e30)
            l_rec[slot] = jnp.zeros_like(l_rec[slot])
            w_rec[slot] = jnp.zeros_like(w_rec[slot])

    blocks = k_scales.shape[0]
    block = tokens // blocks

    def scale_codes(index, part, scales):
        loads[index].wait()
        for place in range(blocks):
            span = pl.ds(place * block, block)
            scale = scales[slot_in[0, place]]
            data[OWN, part, span, :] = (codes[index, span, :].astype(jnp.float32) * scale).astype(jnp.bfloat16)

    sent = []

    def send(part, source, way):
        target = lands(source, way)
        index = len([other for other in sent[:sent.index((part, source, way))] if other[0] == part])
        return pltpu.make_async_remote_copy(
            src_ref=data.at[source, part],
            dst_ref=data.at[target, part],
            send_sem=send_sem.at[part, index],
            recv_sem=recv_sem.at[part, target],
            device_id=device(way),
            device_id_type=MESH,
        )

    def condition(source, way):
        ok = valid(names[source] + way)
        if way == "C" and source in (AM, AZ):
            ok = inner if ok is None else ok & inner
        if way == "C" and source in (BM, BZ):
            ok = outer if ok is None else ok & outer
        return ok

    def push(part, source, way, only=None):
        if (part, source, way) not in sent:
            sent.append((part, source, way))
        ok = condition(source, way)
        if only is not None:
            ok = only if ok is None else ok & only
        guard(ok, lambda: send(part, source, way).start())

    def arrive(part, slot):
        copy = pltpu.make_async_remote_copy(
            src_ref=data.at[slot, part],
            dst_ref=data.at[slot, part],
            send_sem=send_sem.at[part, 0],
            recv_sem=recv_sem.at[part, slot],
            device_id=device(names[slot]),
            device_id_type=MESH,
        )
        guard(valid(names[slot]), copy.wait_recv)

    def relay(part, slot):
        arrive(part, slot)
        if slot in (AM, AZ, BM, BZ):
            push(part, slot, "C")
        if slot in (AM, AZ) and part in (KEY, QUERY):
            push(part, slot, "X")
        if slot == X and part in (VALUE, GRAD):
            push(part, slot, "M")
            push(part, slot, "Z")

    starts, total = [], 0
    for tile in range(tiles):
        first, last = near_range(tile, tiles)
        starts.append(total)
        total += last - first

    def columns(tile):
        first, last = near_range(tile, tiles)
        return first, last, pl.ds(tile * TILE_TOKENS, TILE_TOKENS), pl.ds(starts[tile], last - first)

    units = [
        (tile, start, pl.ds(starts[tile] + start - near_range(tile, tiles)[0], TILE_TOKENS))
        for tile in range(tiles)
        for start in range(*near_range(tile, tiles), TILE_TOKENS)
    ]

    def mix(*strands):
        marks = sorted(
            ((place + 0.5) / len(steps), which, place)
            for which, steps in enumerate(strands)
            for place in range(len(steps))
        )
        for _, which, place in marks:
            strands[which][place]()

    def op_s(slot):
        def unit(tile, start, place):
            own = pl.ds(tile * TILE_TOKENS, TILE_TOKENS)
            e_all[slot, place, :] = dot_nt(data[slot, KEY, start:start + TILE_TOKENS, :], data[OWN, QUERY, own, :])

        return [functools.partial(unit, *item) for item in units]

    def op_d(slot):
        def unit(tile, start, place):
            own = pl.ds(tile * TILE_TOKENS, TILE_TOKENS)
            dp_all[slot, place, :] = dot_nt(data[slot, VALUE, start:start + TILE_TOKENS, :], data[OWN, GRAD, own, :])

        return [functools.partial(unit, *item) for item in units]

    def op_e(slot):
        held = {}

        def top(tile, start, place):
            new = jnp.max(e_all[slot, place, :], axis=0, keepdims=True)
            held[tile] = new if tile not in held else jnp.maximum(held[tile], new)

        def power(tile, start, place, last):
            if ("top", tile) not in held:
                held["top", tile] = held[tile] * LOG2_SCALE
            e = jnp.exp2(e_all[slot, place, :] * LOG2_SCALE - held["top", tile])
            added = jnp.sum(e, axis=0, keepdims=True)
            held["sum", tile] = added if ("sum", tile) not in held else held["sum", tile] + added
            e_all[slot, place, :] = e
            if last:
                own = pl.ds(tile * TILE_TOKENS, TILE_TOKENS)
                m_rec[slot, :, own] = masked(slot, held["top", tile], -1e30)
                l_rec[slot, :, own] = masked(slot, held["sum", tile], 0.0)

        steps = []
        for tile in range(tiles):
            mine = [item for item in units if item[0] == tile]
            steps += [functools.partial(top, *item) for item in mine]
            steps += [functools.partial(power, *item, item is mine[-1]) for item in mine]
        return steps

    def op_w(slot):
        held = {}

        def unit(tile, start, place):
            added = jnp.sum(e_all[slot, place, :] * dp_all[slot, place, :], axis=0, keepdims=True)
            held[tile] = added if tile not in held else held[tile] + added
            if start + TILE_TOKENS == near_range(tile, tiles)[1]:
                w_rec[slot, :, pl.ds(tile * TILE_TOKENS, TILE_TOKENS)] = masked(slot, held[tile], 0.0)

        return [functools.partial(unit, *item) for item in units]

    def stats_send(slot):
        back = {C: C, X: X, MX: ZX, ZX: MX}.get(slot)
        if slot in (AM, BM):
            back = jnp.where(inner, AZ, BZ)
        if slot in (AZ, BZ):
            back = jnp.where(inner, AM, BM)
        return pltpu.make_async_remote_copy(
            src_ref=stats.at[OWN],
            dst_ref=stats.at[back],
            send_sem=st_send.at[slot],
            recv_sem=st_recv.at[back],
            device_id=device(names[slot]),
            device_id_type=MESH,
        )

    def op_total():
        top = m_rec[OWN]
        for slot in range(1, SLOTS):
            top = jnp.maximum(top, m_rec[slot])
        total = l_rec[OWN] * jnp.exp2(m_rec[OWN] - top)
        weighed = w_rec[OWN] * jnp.exp2(m_rec[OWN] - top)
        for slot in range(1, SLOTS):
            factor = jnp.exp2(m_rec[slot] - top)
            total += l_rec[slot] * factor
            weighed += w_rec[slot] * factor
        stats[OWN, 0:1, :] = top + jnp.log2(total)
        stats[OWN, 1:2, :] = weighed / total

    def op_q(slot, to):
        held = {}

        def unit(tile, start, place):
            own = pl.ds(tile * TILE_TOKENS, TILE_TOKENS)
            rows_of = pl.ds(start, TILE_TOKENS)
            if tile not in held:
                held[tile] = jnp.exp2(m_rec[slot, :, own] - stats[OWN, 0:1, own])
            if ("turned", start) not in held:
                held["turned", start] = data[slot, KEY, rows_of, :].T
            prob = e_all[slot, place, :] * held[tile]
            dscore = (prob * (dp_all[slot, place, :] - stats[OWN, 1:2, own])).astype(jnp.bfloat16)
            if to is not None:
                ps[to, rows_of, own] = prob.astype(jnp.bfloat16)
                ds[to, rows_of, own] = dscore
            added = jnp.dot(held["turned", start], dscore, preferred_element_type=jnp.float32)
            held["sum", tile] = added if ("sum", tile) not in held else held["sum", tile] + added
            if start + TILE_TOKENS == near_range(tile, tiles)[1]:
                if slot == OWN:
                    dq_acc[:, own] = held["sum", tile]
                else:
                    dq_acc[:, own] += across(slot, held["sum", tile])

        return [functools.partial(unit, *item) for item in units]

    def op_ks(slot):
        def unit(index, tile, start, place):
            own, near = pl.ds(tile * TILE_TOKENS, TILE_TOKENS), pl.ds(start, TILE_TOKENS)
            held = pl.ds(index * TILE_TOKENS, TILE_TOKENS)
            e_all[slot, held, :] = dot_nt(data[OWN, KEY, own, :], data[slot, QUERY, near, :])

        return [functools.partial(unit, index, *item) for index, item in enumerate(units)]

    def op_kd(slot):
        def unit(index, tile, start, place):
            own, near = pl.ds(tile * TILE_TOKENS, TILE_TOKENS), pl.ds(start, TILE_TOKENS)
            held = pl.ds(index * TILE_TOKENS, TILE_TOKENS)
            dp_all[slot, held, :] = dot_nt(data[OWN, VALUE, own, :], data[slot, GRAD, near, :])

        return [functools.partial(unit, index, *item) for index, item in enumerate(units)]

    def op_kv(slot, to):
        def unit(index, tile, start, place):
            own, near = pl.ds(tile * TILE_TOKENS, TILE_TOKENS), pl.ds(start, TILE_TOKENS)
            held = pl.ds(index * TILE_TOKENS, TILE_TOKENS)
            prob = jnp.exp2(e_all[slot, held, :] * LOG2_SCALE - stats[slot, 0:1, near])
            ps[to, own, near] = prob.astype(jnp.bfloat16)
            ds[to, own, near] = (prob * (dp_all[slot, held, :] - stats[slot, 1:2, near])).astype(jnp.bfloat16)

        return [functools.partial(unit, index, *item) for index, item in enumerate(units)]

    def op_m(slot, source):
        queries_of = OWN if slot == C else slot
        held = {}

        def unit(which, tile):
            part, right, acc = ((QUERY, ds, dk_acc), (GRAD, ps, dv_acc))[which]
            first, last, own, place = columns(tile)
            if which not in held:
                held[which] = data[queries_of, part].T
            summed = dot_nt(held[which][:, first:last], right[source, own, first:last])
            if part == QUERY:
                summed = summed * INVERSE
            rounded = summed.astype(jnp.bfloat16)
            if slot == C:
                part_out[which, :, own] = rounded
            elif slot == OWN:
                acc[:, own] = rounded.astype(jnp.float32)
            else:
                acc[:, own] += across(slot, rounded.astype(jnp.float32))

        return [functools.partial(unit, which, tile) for tile in range(tiles) for which in range(2)]

    def parts_send():
        return pltpu.make_async_remote_copy(
            src_ref=part_out, dst_ref=part_in, send_sem=pt_send, recv_sem=pt_recv,
            device_id=device("C"), device_id_type=MESH,
        )

    def stats_arrive(slot):
        copy = pltpu.make_async_remote_copy(
            src_ref=stats.at[slot], dst_ref=stats.at[slot], send_sem=st_send.at[slot], recv_sem=st_recv.at[slot],
            device_id=device(names[slot]), device_id_type=MESH,
        )
        guard(valid(names[slot]), copy.wait_recv)

    scale_codes(0, KEY, k_scales)
    pl.semaphore_wait(barrier, count)
    push(KEY, OWN, "M", inner)
    push(KEY, OWN, "Z", inner)
    scale_codes(1, VALUE, v_scales)
    push(VALUE, OWN, "C")
    push(KEY, OWN, "X")
    push(KEY, OWN, "C")
    push(VALUE, OWN, "X")
    arrive(VALUE, C)
    loads[3].wait()
    loads[2].wait()
    mix(op_d(C), op_s(OWN))

    mix(op_d(OWN))

    push(KEY, OWN, "M", outer)
    push(KEY, OWN, "Z", outer)
    push(VALUE, OWN, "M", outer)
    push(VALUE, OWN, "Z", outer)
    push(GRAD, OWN, "X")
    relay(KEY, AM)
    relay(KEY, AZ)
    relay(VALUE, X)
    push(VALUE, OWN, "M", inner)
    push(VALUE, OWN, "Z", inner)
    arrive(KEY, X)
    mix(op_s(X), op_s(AM))

    push(QUERY, OWN, "M", inner)
    push(QUERY, OWN, "Z", inner)
    relay(KEY, BZ)
    arrive(KEY, C)
    mix(op_s(BZ), op_s(C), op_s(AZ))

    relay(KEY, BM)
    mix(op_e(C), op_e(AZ), op_e(AM), op_s(BM))

    mix(op_e(OWN), op_e(BM))

    push(QUERY, OWN, "X")
    relay(VALUE, BM)
    push(GRAD, OWN, "M", inner)
    push(GRAD, OWN, "Z", inner)
    mix(op_e(X), op_w(OWN), op_d(BM), op_d(X))

    relay(VALUE, BZ)
    arrive(VALUE, MX)
    mix(op_e(BZ), op_w(BM), op_w(X), op_d(MX))

    arrive(KEY, ZX)
    arrive(VALUE, ZX)
    inner_rows(lambda: mix(op_s(ZX), op_d(ZX)))

    relay(GRAD, X)
    arrive(KEY, MX)
    mix(op_e(ZX), op_d(BZ), op_s(MX))

    relay(VALUE, AM)
    relay(VALUE, AZ)
    mix(op_e(MX), op_w(BZ), op_d(AM), op_d(AZ))

    mix(op_w(ZX), op_w(C), op_w(AZ), op_w(MX))

    mix(op_w(AM))

    push(GRAD, OWN, "M", outer)
    push(GRAD, OWN, "Z", outer)
    op_total()
    relay(QUERY, AM)
    relay(QUERY, AZ)
    mix(op_q(OWN, 0), op_q(AM, None))

    push(QUERY, OWN, "M", outer)
    push(QUERY, OWN, "Z", outer)
    mix(op_q(BM, None), op_q(AZ, None), op_m(OWN, 0))

    for slot in range(1, SLOTS):
        if slot != C:
            guard(valid(names[slot]), stats_send(slot).start)
    mix(op_q(BZ, None), op_q(C, 0), op_q(X, None), op_ks(AZ))

    relay(GRAD, AM)
    arrive(QUERY, X)
    mix(op_q(MX, None), op_kd(AM), op_ks(X), op_ks(AM))

    relay(GRAD, AZ)
    arrive(GRAD, MX)
    inner_rows(lambda: mix(op_q(ZX, None), op_kd(MX), op_kd(X)))

    arrive(QUERY, MX)
    stats_arrive(X)
    inner_rows(lambda: mix(op_kv(X, 1), op_ks(MX)))

    stats_arrive(AM)
    mix(op_kv(AM, 2), op_m(C, 0), op_kd(AZ))

    arrive(GRAD, ZX)
    stats_arrive(MX)
    arrive(QUERY, ZX)
    inner_rows(lambda: mix(op_kv(MX, 0), op_kd(ZX), op_ks(ZX), op_m(X, 1)))

    stats_arrive(ZX)
    inner_rows(lambda: mix(op_kv(ZX, 1), op_m(MX, 0)))

    relay(GRAD, BM)
    relay(GRAD, BZ)
    parts_send().start()
    stats_arrive(AZ)
    mix(op_kv(AZ, 0), op_m(AM, 2), op_kd(BZ), op_m(ZX, 1))

    relay(QUERY, BZ)
    relay(QUERY, BM)
    mix(op_ks(BZ), op_ks(BM), op_kd(BM))

    stats_arrive(BZ)
    stats_arrive(BM)
    mix(op_kv(BZ, 2), op_kv(BM, 1))

    parts_send().wait_recv()
    mix(op_m(BZ, 2), op_m(AZ, 0), op_m(BM, 1))

    dq_out[...] = (dq_acc[...] * INVERSE).astype(dq_out.dtype).T
    dk_out[...] = (dk_acc[...] + part_in[0].astype(jnp.float32)).astype(dk_out.dtype).T
    dv_out[...] = (dv_acc[...] + part_in[1].astype(jnp.float32)).astype(dv_out.dtype).T

    for key in sent:
        guard(condition(*key[1:]), send(*key).wait_send)
    for slot in range(1, SLOTS):
        if slot != C:
            guard(valid(names[slot]), stats_send(slot).wait_send)
    parts_send().wait_send()


def put_out(dq_in, dk_in, dv_in, dq_out, dk_out, dv_out, out_sem):
    pairs = ((dq_in, dq_out), (dk_in, dk_out), (dv_in, dv_out))
    stores = [pltpu.make_async_copy(pair[0], pair[1], out_sem.at[i]) for i, pair in enumerate(pairs)]
    for store in stores:
        store.start()
    for store in stores:
        store.wait()


def per_device(queries, key_codes, value_codes, key_scales, value_scales, scale_slot, grad_out):
    rows = ROW_TILES
    frames = lax.axis_size("tm") // rows
    tokens, head_dim = queries.shape
    tiles = tokens // TILE_TOKENS
    near = sum(near_range(tile, tiles)[1] - near_range(tile, tiles)[0] for tile in range(tiles))
    shape = jax.ShapeDtypeStruct((tokens, head_dim), jnp.bfloat16)
    grads = pl.pallas_call(
        functools.partial(kernel, frames, rows),
        out_shape=(pltpu.VMEM((tokens, head_dim), jnp.bfloat16),) * 3,
        in_specs=[pl.BlockSpec(memory_space=pltpu.HBM)] * 4 + [pl.BlockSpec(memory_space=pltpu.SMEM)] * 3,
        out_specs=[pl.BlockSpec(memory_space=pltpu.VMEM)] * 3,
        scratch_shapes=[
            pltpu.VMEM((SLOTS, 4, tokens, head_dim), jnp.bfloat16),
            pltpu.VMEM((2, tokens, head_dim), jnp.bfloat16),
            pltpu.VMEM((SLOTS, 2, tokens), jnp.float32),
            pltpu.VMEM((SLOTS, near, TILE_TOKENS), jnp.float32),
            pltpu.VMEM((SLOTS, near, TILE_TOKENS), jnp.float32),
            pltpu.VMEM((3, tokens, tokens), jnp.bfloat16),
            pltpu.VMEM((3, tokens, tokens), jnp.bfloat16),
            pltpu.VMEM((SLOTS, 1, tokens), jnp.float32),
            pltpu.VMEM((SLOTS, 1, tokens), jnp.float32),
            pltpu.VMEM((SLOTS, 1, tokens), jnp.float32),
            pltpu.VMEM((head_dim, tokens), jnp.float32),
            pltpu.VMEM((head_dim, tokens), jnp.float32),
            pltpu.VMEM((head_dim, tokens), jnp.float32),
            pltpu.VMEM((2, head_dim, tokens), jnp.bfloat16),
            pltpu.VMEM((2, head_dim, tokens), jnp.bfloat16),
            pltpu.SemaphoreType.DMA((4,)),
            pltpu.SemaphoreType.DMA((4, 10)),
            pltpu.SemaphoreType.DMA((4, SLOTS)),
            pltpu.SemaphoreType.DMA((SLOTS,)),
            pltpu.SemaphoreType.DMA((SLOTS,)),
            pltpu.SemaphoreType.DMA,
            pltpu.SemaphoreType.DMA,
        ],
        compiler_params=pltpu.CompilerParams(
            collective_id=0, has_side_effects=True, vmem_limit_bytes=60 * 1024 * 1024
        ),
    )(queries, key_codes, value_codes, grad_out, key_scales, value_scales, scale_slot)
    return tuple(pl.pallas_call(
        put_out,
        out_shape=(shape, shape, shape),
        in_specs=[pl.BlockSpec(memory_space=pltpu.VMEM)] * 3,
        out_specs=[pl.BlockSpec(memory_space=pl.ANY)] * 3,
        scratch_shapes=[pltpu.SemaphoreType.DMA((3,))],
        compiler_params=pltpu.CompilerParams(vmem_limit_bytes=2 * 1024 * 1024),
    )(*grads))


def solution(mesh):
    in_specs = (
        P(("grp", "tm"), None),
        P(("grp", "tm"), None),
        P(("grp", "tm"), None),
        P(("grp", "tm")),
        P(("grp", "tm")),
        P(("grp", "tm"), None),
        P(("grp", "tm"), None),
    )
    out_specs = (P(("grp", "tm"), None), P(("grp", "tm"), None), P(("grp", "tm"), None))
    return jax.shard_map(
        per_device, mesh=mesh, in_specs=in_specs, out_specs=out_specs, check_vma=False
    )
```

time: 37.5 us -> 39.8 us (1.061)
  Pallas kernels: 36.7 us -> 38.8 us
    pallas_call x1, Pallas kernels: 35.9 us -> 37.9 us  [per_device(): pl.pallas_call(functools.partial(kernel, frames, rows), out_shape=(pltpu....]
where the time goes in v2:
time: 39.8 us; the launch traced here: 39.6 us
  Pallas kernels  38.8 us (97%)
  between operations  0.82 us (2%)
    pallas_call x1, Pallas kernels, per_device(): pl.pallas_call(functools.partial(kernel, frames, rows), out_shape=(pltpu....  37.9 us
    pallas_call x1, Pallas kernels, per_device(): pl.pallas_call(put_out, out_shape=(shape, shape, shape), in_specs=[pl.Blo...  0.83 us

profile of v2, /device:TPU:9, one launch (start us, length us, event | category | flops | bytes accessed | tf_op | source)
XLA Modules:
  0.0 39.6 jit_solution(15201406584742330527)
XLA Ops:
  0.6 37.9 %shard_map.94 = (bf16[768,128]{1,0:T(8,128)(2,1)S(1)}, bf16[768,128]{1,0:T(8,128)(2,1)S(1)}, bf16[768,128]{1,0:T(8,128)(2,1)S(1)}) custom-call(bf16[768,128]{1,0:T(8,128)(2,1)} %q_in.1, bf16[768,128]{1,0:T(8,128)(2,1)} %k_in.1, bf16[768,128]{1,0:T(8,128)(2,1)} %v_in.1, bf16[768,128]{1,0:T(8,128)(2,1)} %g_in.1, f32[6]{0:T(128)} %k_scales.1, f32[6]{0:T(128)} %v_scales.1, ...), custom_call_target="tpu_custom_call" | custom-call | tf_op jit(solution)/shard_map/pallas_call | solution.py:522
  38.6 0.8 %shard_map.95 = (bf16[768,128]{1,0:T(8,128)(2,1)}, bf16[768,128]{1,0:T(8,128)(2,1)}, bf16[768,128]{1,0:T(8,128)(2,1)}) custom-call(bf16[768,128]{1,0:T(8,128)(2,1)S(1)} %get-tuple-element.6.dq_in, bf16[768,128]{1,0:T(8,128)(2,1)S(1)} %get-tuple-element.7.dk_in, bf16[768,128]{1,0:T(8,128)(2,1)S(1)} %get-tuple-element.8.dv_in), custom_call_target="tpu_custom_call" | custom-call | tf_op jit(solution)/shard_map/pallas_call | solution.py:555

commit v3 on v2

--- a/solution.py
+++ b/solution.py
@@ -103,6 +103,9 @@
             pl.semaphore_signal(barrier, inc=1, device_id=device(names[slot]), device_id_type=MESH)
 
         guard(ok, greet)
+
+    for acc in (dq_acc, dk_acc, dv_acc):
+        acc[...] = jnp.zeros_like(acc)
 
     for name, slots in (("M", (AM, BM)), ("Z", (AZ, BZ))):
         @pl.when(jnp.logical_not(has[name]))
@@ -205,9 +208,16 @@
             strands[which][place]()
 
     def op_s(slot):
+        held = {}
+
         def unit(tile, start, place):
             own = pl.ds(tile * TILE_TOKENS, TILE_TOKENS)
-            e_all[slot, place, :] = dot_nt(data[slot, KEY, start:start + TILE_TOKENS, :], data[OWN, QUERY, own, :])
+            scores = dot_nt(data[slot, KEY, start:start + TILE_TOKENS, :], data[OWN, QUERY, own, :]) * LOG2_SCALE
+            e_all[slot, place, :] = scores
+            new = jnp.max(scores, axis=0, keepdims=True)
+            held[tile] = new if tile not in held else jnp.maximum(held[tile], new)
+            if start + TILE_TOKENS == near_range(tile, tiles)[1]:
+                m_rec[slot, :, own] = held[tile]
 
         return [functools.partial(unit, *item) for item in units]
 
@@ -221,28 +231,19 @@
     def op_e(slot):
         held = {}
 
-        def top(tile, start, place):
-            new = jnp.max(e_all[slot, place, :], axis=0, keepdims=True)
-            held[tile] = new if tile not in held else jnp.maximum(held[tile], new)
-
-        def power(tile, start, place, last):
+        def unit(tile, start, place):
+            own = pl.ds(tile * TILE_TOKENS, TILE_TOKENS)
             if ("top", tile) not in held:
-                held["top", tile] = held[tile] * LOG2_SCALE
-            e = jnp.exp2(e_all[slot, place, :] * LOG2_SCALE - held["top", tile])
+                held["top", tile] = m_rec[slot, :, own]
+            e = jnp.exp2(e_all[slot, place, :] - held["top", tile])
             added = jnp.sum(e, axis=0, keepdims=True)
-            held["sum", tile] = added if ("sum", tile) not in held else held["sum", tile] + added
+            held[tile] = added if tile not in held else held[tile] + added
             e_all[slot, place, :] = e
-            if last:
-                own = pl.ds(tile * TILE_TOKENS, TILE_TOKENS)
+            if start + TILE_TOKENS == near_range(tile, tiles)[1]:
                 m_rec[slot, :, own] = masked(slot, held["top", tile], -1e30)
-                l_rec[slot, :, own] = masked(slot, held["sum", tile], 0.0)
-
-        steps = []
-        for tile in range(tiles):
-            mine = [item for item in units if item[0] == tile]
-            steps += [functools.partial(top, *item) for item in mine]
-            steps += [functools.partial(power, *item, item is mine[-1]) for item in mine]
-        return steps
+                l_rec[slot, :, own] = masked(slot, held[tile], 0.0)
+
+        return [functools.partial(unit, *item) for item in units]
 
     def op_w(slot):
         held = {}
@@ -301,10 +302,7 @@
             added = jnp.dot(held["turned", start], dscore, preferred_element_type=jnp.float32)
             held["sum", tile] = added if ("sum", tile) not in held else held["sum", tile] + added
             if start + TILE_TOKENS == near_range(tile, tiles)[1]:
-                if slot == OWN:
-                    dq_acc[:, own] = held["sum", tile]
-                else:
-                    dq_acc[:, own] += across(slot, held["sum", tile])
+                dq_acc[:, own] += across(slot, held["sum", tile])
 
         return [functools.partial(unit, *item) for item in units]
 
@@ -312,7 +310,8 @@
         def unit(index, tile, start, place):
             own, near = pl.ds(tile * TILE_TOKENS, TILE_TOKENS), pl.ds(start, TILE_TOKENS)
             held = pl.ds(index * TILE_TOKENS, TILE_TOKENS)
-            e_all[slot, held, :] = dot_nt(data[OWN, KEY, own, :], data[slot, QUERY, near, :])
+            scores = dot_nt(data[OWN, KEY, own, :], data[slot, QUERY, near, :])
+            e_all[slot, held, :] = scores * LOG2_SCALE
 
         return [functools.partial(unit, index, *item) for index, item in enumerate(units)]
 
@@ -328,7 +327,7 @@
         def unit(index, tile, start, place):
             own, near = pl.ds(tile * TILE_TOKENS, TILE_TOKENS), pl.ds(start, TILE_TOKENS)
             held = pl.ds(index * TILE_TOKENS, TILE_TOKENS)
-            prob = jnp.exp2(e_all[slot, held, :] * LOG2_SCALE - stats[slot, 0:1, near])
+            prob = jnp.exp2(e_all[slot, held, :] - stats[slot, 0:1, near])
             ps[to, own, near] = prob.astype(jnp.bfloat16)
             ds[to, own, near] = (prob * (dp_all[slot, held, :] - stats[slot, 1:2, near])).astype(jnp.bfloat16)
 
@@ -349,8 +348,6 @@
             rounded = summed.astype(jnp.bfloat16)
             if slot == C:
                 part_out[which, :, own] = rounded
-            elif slot == OWN:
-                acc[:, own] = rounded.astype(jnp.float32)
             else:
                 acc[:, own] += across(slot, rounded.astype(jnp.float32))
 
@@ -371,127 +368,125 @@
 
     scale_codes(0, KEY, k_scales)
     pl.semaphore_wait(barrier, count)
+    push(KEY, OWN, "X")
     push(KEY, OWN, "M", inner)
     push(KEY, OWN, "Z", inner)
+    push(KEY, OWN, "C")
     scale_codes(1, VALUE, v_scales)
+    push(VALUE, OWN, "X")
     push(VALUE, OWN, "C")
-    push(KEY, OWN, "X")
-    push(KEY, OWN, "C")
-    push(VALUE, OWN, "X")
-    arrive(VALUE, C)
-    loads[3].wait()
+    arrive(KEY, X)
     loads[2].wait()
-    mix(op_d(C), op_s(OWN))
-
-    mix(op_d(OWN))
+    arrive(KEY, C)
+    mix(op_s(X), op_s(C))
 
     push(KEY, OWN, "M", outer)
     push(KEY, OWN, "Z", outer)
     push(VALUE, OWN, "M", outer)
     push(VALUE, OWN, "Z", outer)
-    push(GRAD, OWN, "X")
+    relay(KEY, AZ)
+    mix(op_s(OWN))
+
     relay(KEY, AM)
-    relay(KEY, AZ)
-    relay(VALUE, X)
     push(VALUE, OWN, "M", inner)
     push(VALUE, OWN, "Z", inner)
-    arrive(KEY, X)
-    mix(op_s(X), op_s(AM))
+    relay(VALUE, X)
+    loads[3].wait()
+    inner_rows(lambda: mix(op_e(X), op_d(X)))
 
     push(QUERY, OWN, "M", inner)
     push(QUERY, OWN, "Z", inner)
-    relay(KEY, BZ)
-    arrive(KEY, C)
-    mix(op_s(BZ), op_s(C), op_s(AZ))
+    mix(op_e(C), op_s(AM))
 
     relay(KEY, BM)
-    mix(op_e(C), op_e(AZ), op_e(AM), op_s(BM))
-
-    mix(op_e(OWN), op_e(BM))
-
-    push(QUERY, OWN, "X")
-    relay(VALUE, BM)
     push(GRAD, OWN, "M", inner)
     push(GRAD, OWN, "Z", inner)
-    mix(op_e(X), op_w(OWN), op_d(BM), op_d(X))
+    arrive(VALUE, C)
+    mix(op_e(AM), op_d(C), op_s(BM), op_s(AZ))
+
+    push(GRAD, OWN, "X")
+    relay(KEY, BZ)
+    mix(op_e(BM), op_e(AZ), op_d(OWN), op_s(BZ))
+
+    relay(VALUE, BM)
+    push(QUERY, OWN, "X")
+    arrive(KEY, ZX)
+    mix(op_e(BZ), op_d(BM), op_s(ZX))
 
     relay(VALUE, BZ)
+    relay(VALUE, AZ)
+    relay(VALUE, AM)
+    arrive(KEY, MX)
+    mix(op_e(OWN), op_d(AZ), op_s(MX), op_d(BZ))
+
+    mix(op_e(MX), op_w(OWN))
+
+    arrive(VALUE, ZX)
+    mix(op_e(ZX), op_w(X), op_d(ZX), op_d(AM))
+
+    relay(GRAD, X)
     arrive(VALUE, MX)
-    mix(op_e(BZ), op_w(BM), op_w(X), op_d(MX))
-
-    arrive(KEY, ZX)
-    arrive(VALUE, ZX)
-    inner_rows(lambda: mix(op_s(ZX), op_d(ZX)))
-
-    relay(GRAD, X)
-    arrive(KEY, MX)
-    mix(op_e(ZX), op_d(BZ), op_s(MX))
-
-    relay(VALUE, AM)
-    relay(VALUE, AZ)
-    mix(op_e(MX), op_w(BZ), op_d(AM), op_d(AZ))
-
-    mix(op_w(ZX), op_w(C), op_w(AZ), op_w(MX))
-
-    mix(op_w(AM))
-
+    mix(op_w(BM), op_w(BZ), op_w(ZX), op_d(MX))
+
+    push(QUERY, OWN, "M", outer)
+    push(QUERY, OWN, "Z", outer)
     push(GRAD, OWN, "M", outer)
     push(GRAD, OWN, "Z", outer)
+    relay(QUERY, AM)
+    mix(op_w(C), op_w(AZ), op_w(AM), op_w(MX))
+
     op_total()
-    relay(QUERY, AM)
-    relay(QUERY, AZ)
-    mix(op_q(OWN, 0), op_q(AM, None))
-
-    push(QUERY, OWN, "M", outer)
-    push(QUERY, OWN, "Z", outer)
-    mix(op_q(BM, None), op_q(AZ, None), op_m(OWN, 0))
-
     for slot in range(1, SLOTS):
         if slot != C:
             guard(valid(names[slot]), stats_send(slot).start)
-    mix(op_q(BZ, None), op_q(C, 0), op_q(X, None), op_ks(AZ))
+    relay(QUERY, AZ)
+    mix(op_q(OWN, 0), op_q(AM, None), op_q(AZ, None))
 
     relay(GRAD, AM)
+    mix(op_q(X, None), op_q(C, 1), op_kd(AM), op_ks(AM))
+
+    relay(GRAD, AZ)
+    inner_rows(lambda: mix(op_q(ZX, None), op_q(MX, None), op_kd(X)))
+
+    stats_arrive(AM)
     arrive(QUERY, X)
-    mix(op_q(MX, None), op_kd(AM), op_ks(X), op_ks(AM))
-
-    relay(GRAD, AZ)
+    mix(op_kv(AM, 2), op_m(OWN, 0), op_ks(X), op_m(C, 1))
+
+    arrive(GRAD, ZX)
+    mix(op_q(BZ, None), op_kd(AZ), op_kd(ZX), op_m(AM, 2))
+
+    arrive(QUERY, MX)
     arrive(GRAD, MX)
-    inner_rows(lambda: mix(op_q(ZX, None), op_kd(MX), op_kd(X)))
-
-    arrive(QUERY, MX)
     stats_arrive(X)
-    inner_rows(lambda: mix(op_kv(X, 1), op_ks(MX)))
-
-    stats_arrive(AM)
-    mix(op_kv(AM, 2), op_m(C, 0), op_kd(AZ))
-
-    arrive(GRAD, ZX)
+    inner_rows(lambda: mix(op_kv(X, 0), op_ks(MX), op_kd(MX)))
+
     stats_arrive(MX)
     arrive(QUERY, ZX)
-    inner_rows(lambda: mix(op_kv(MX, 0), op_kd(ZX), op_ks(ZX), op_m(X, 1)))
-
-    stats_arrive(ZX)
-    inner_rows(lambda: mix(op_kv(ZX, 1), op_m(MX, 0)))
-
-    relay(GRAD, BM)
-    relay(GRAD, BZ)
+    inner_rows(lambda: mix(op_kv(MX, 1), op_m(X, 0), op_ks(ZX)))
+
+    relay(QUERY, BM)
+    mix(op_q(BM, None), op_ks(AZ))
+    dq_out[...] = (dq_acc[...] * INVERSE).astype(dq_out.dtype).T
+
+    relay(QUERY, BZ)
     parts_send().start()
     stats_arrive(AZ)
-    mix(op_kv(AZ, 0), op_m(AM, 2), op_kd(BZ), op_m(ZX, 1))
-
-    relay(QUERY, BZ)
-    relay(QUERY, BM)
-    mix(op_ks(BZ), op_ks(BM), op_kd(BM))
-
+    mix(op_kv(AZ, 0), op_ks(BZ), op_ks(BM), op_m(MX, 1))
+
+    relay(GRAD, BZ)
+    stats_arrive(ZX)
+    mix(op_kv(ZX, 1), op_kd(BZ))
+
+    relay(GRAD, BM)
     stats_arrive(BZ)
+    mix(op_kv(BZ, 2), op_kd(BM), op_m(ZX, 1))
+
     stats_arrive(BM)
-    mix(op_kv(BZ, 2), op_kv(BM, 1))
+    mix(op_kv(BM, 1), op_m(BZ, 2))
+
+    mix(op_m(BM, 1), op_m(AZ, 0))
 
     parts_send().wait_recv()
-    mix(op_m(BZ, 2), op_m(AZ, 0), op_m(BM, 1))
-
-    dq_out[...] = (dq_acc[...] * INVERSE).astype(dq_out.dtype).T
     dk_out[...] = (dk_acc[...] + part_in[0].astype(jnp.float32)).astype(dk_out.dtype).T
     dv_out[...] = (dv_acc[...] + part_in[1].astype(jnp.float32)).astype(dv_out.dtype).T
 

time: 39.8 us -> 36.3 us (0.912)
  Pallas kernels: 38.8 us -> 35.2 us
    pallas_call x1, Pallas kernels: 37.9 us -> 34.4 us  [per_device(): pl.pallas_call(functools.partial(kernel, frames, rows), out_shape=(pltpu....]
where the time goes in v3:
time: 36.3 us; the launch traced here: 36 us
  Pallas kernels  35.2 us (97%)
  between operations  0.8 us (2%)
    pallas_call x1, Pallas kernels, per_device(): pl.pallas_call(functools.partial(kernel, frames, rows), out_shape=(pltpu....  34.4 us
    pallas_call x1, Pallas kernels, per_device(): pl.pallas_call(put_out, out_shape=(shape, shape, shape), in_specs=[pl.Blo...  0.83 us

profile of v3, /device:TPU:9, one launch (start us, length us, event | category | flops | bytes accessed | tf_op | source)
XLA Modules:
  0.0 36.0 jit_solution(502529562888282553)
XLA Ops:
  0.6 34.4 %shard_map.94 = (bf16[768,128]{1,0:T(8,128)(2,1)S(1)}, bf16[768,128]{1,0:T(8,128)(2,1)S(1)}, bf16[768,128]{1,0:T(8,128)(2,1)S(1)}) custom-call(bf16[768,128]{1,0:T(8,128)(2,1)} %q_in.1, bf16[768,128]{1,0:T(8,128)(2,1)} %k_in.1, bf16[768,128]{1,0:T(8,128)(2,1)} %v_in.1, bf16[768,128]{1,0:T(8,128)(2,1)} %g_in.1, f32[6]{0:T(128)} %k_scales.1, f32[6]{0:T(128)} %v_scales.1, ...), custom_call_target="tpu_custom_call" | custom-call | tf_op jit(solution)/shard_map/pallas_call | solution.py:517
  35.0 0.8 %shard_map.95 = (bf16[768,128]{1,0:T(8,128)(2,1)}, bf16[768,128]{1,0:T(8,128)(2,1)}, bf16[768,128]{1,0:T(8,128)(2,1)}) custom-call(bf16[768,128]{1,0:T(8,128)(2,1)S(1)} %get-tuple-element.6.dq_in, bf16[768,128]{1,0:T(8,128)(2,1)S(1)} %get-tuple-element.7.dk_in, bf16[768,128]{1,0:T(8,128)(2,1)S(1)} %get-tuple-element.8.dv_in), custom_call_target="tpu_custom_call" | custom-call | tf_op jit(solution)/shard_map/pallas_call | solution.py:550
